TPU v7x, 32 devices: a whole 2x2x4 slice. The times are simulated.
32 devices in a mesh: layer: 2 (over y), row: 4 (over z), col: 4 (over x, core).
Axes of the slice: x: 2, y: 2, z: 4, core: 2. Of those that a mesh axis runs over, the one named last changes fastest.
Arguments:
- leaf_sol: bfloat16 [8, 256, 256], P(('layer', 'col'), 'row'), may hold values from -6 to 6
- lower_blocks: bfloat16 [8192, 1024], P(('layer', 'row'), 'col'), may hold values from -0.1875 to 0.1875
- lower_mask: int32 [32, 4], P(('layer', 'row'), 'col'), may hold values 0 or 1
- upper_blocks: bfloat16 [2048, 4096], P(('layer', 'col'), 'row'), may hold values from -0.125 to 0.125
- upper_mask: int32 [8, 16], P(('layer', 'col'), 'row'), may hold values 0 or 1
- anc_rhs: bfloat16 [4096, 256], P(('row', 'col')), may hold values from -6 to 6
- diag_inv: bfloat16 [4096, 256], P(('row', 'col')), may hold values from -0.375 to 0.375
Outputs:
- new_leaves: bfloat16 [8, 256, 256], P(('layer', 'col'), 'row')
- anc_sol: bfloat16 [4096, 256], P(('row', 'col'))
Inputs may be any that keep to these rules, and one draw needn't show every extreme that they name: `lower_mask`: 1 marks a stored block of L. `upper_mask`: 1 marks a stored block of U.
All inputs are finite; a program needn't handle non-finite values.
Results may differ from a plain program's by a relative error of at most 0.0044.
Values may be sent and summed in bfloat16 or wider, within the bound.
A program may use at most 64 MiB of HBM per device.

v0:
```python
import jax
import jax.numpy as jnp
from jax import lax
from jax.sharding import PartitionSpec as P


def expand(mask, block):
    first, second = mask.shape
    full = jnp.broadcast_to(mask[:, None, :, None], (first, block, second, block))
    return full.reshape(first * block, second * block)


def shards(leaf_sol, lower_blocks, lower_mask, upper_blocks, upper_mask, anc_rhs, diag_inv):
    block = diag_inv.shape[1]
    width = leaf_sol.shape[2]
    lower_masked = lower_blocks * expand(lower_mask, block).astype(jnp.bfloat16)
    upper_masked = upper_blocks * expand(upper_mask, block).astype(jnp.bfloat16)
    columns = lower_masked
    term = lax.dot_general(
        lax.all_gather(leaf_sol, "row", axis=1, tiled=True)[0],
        columns,
        (((0,), (1,)), ((), ())),
        preferred_element_type=jnp.float32,
    )
    inverse = diag_inv.astype(jnp.float32)
    layers = lax.axis_size("layer")
    columns = lax.axis_size("col")
    slice_width = width // layers
    pieces = term.reshape(layers, slice_width, columns, block)
    pieces = pieces.transpose(0, 2, 1, 3).reshape(layers * columns, slice_width, block)
    summed = lax.psum_scatter(pieces, ("layer", "col"), scatter_dimension=0, tiled=True)[0]
    layer_index = lax.axis_index("layer")
    rhs_part = lax.dynamic_slice_in_dim(anc_rhs, layer_index * slice_width, slice_width, 1)
    remain = rhs_part.astype(jnp.float32).T - summed
    solved_part = lax.dot_general(
        remain,
        inverse,
        (((1,), (1,)), ((), ())),
        precision=lax.Precision.HIGHEST,
        preferred_element_type=jnp.float32,
    ).astype(jnp.bfloat16)
    gathered_sides = lax.all_gather(solved_part, "layer", axis=0, tiled=True)
    anc_sol = gathered_sides.T
    columns = upper_masked
    folded = jnp.dot(
        columns,
        lax.all_gather(anc_sol, "col", axis=0, tiled=True),
        preferred_element_type=jnp.float32,
    )
    correct = lax.psum_scatter(folded, "row", scatter_dimension=0, tiled=True)
    new_leaves = (leaf_sol[0].astype(jnp.float32) - correct).astype(jnp.bfloat16)
    return (new_leaves.reshape(leaf_sol.shape), anc_sol)


def solution(mesh):
    in_specs = (
        P(("layer", "col"), "row", None),
        P(("layer", "row"), "col"),
        P(("layer", "row"), "col"),
        P(("layer", "col"), "row"),
        P(("layer", "col"), "row"),
        P(("row", "col"), None),
        P(("row", "col"), None),
    )
    out_specs = (P(("layer", "col"), "row", None), P(("row", "col"), None))
    return jax.shard_map(shards, mesh=mesh, in_specs=in_specs, out_specs=out_specs, check_vma=False)
```

profile of v0, /device:TPU:0, one launch (start us, length us, event | category | flops | bytes accessed | tf_op | source)
XLA Modules:
  0.0 106.7 jit_solution(17108516704674506642)
XLA Ops:
  7.2 0.0 copy-start
  7.2 0.0 reduce-scatter.3.cloned.1.call-start
  7.2 0.7 convert_bitcast_fusion
  7.9 0.1 broadcast_bitcast_fusion
  8.0 15.3 %all_gather.9 = bf16[1,256,256]{2,1,0:T(8,128)(2,1)S(1)} all-gather(bf16[1,64,256]{2,1,0:T(8,128)(2,1)} %param.7), channel_id=1, replica_groups=mesh['layer'=2,'row'=4,'col'=4] {'row'}, dimensions={1}, use_global_device_ids=true | all-gather | bytes 163840 | tf_op jit(solution)/shard_map/all_gather | solution.py:20
  23.3 1.4 %convolution_bitcast_fusion = f32[256,1024]{0,1:T(8,128)S(1)} fusion(bf16[1024,256]{1,0:T(8,128)(2,1)} %param.8, bf16[1024]{0:T(1024)(128)(2,1)S(1)} %bitcast.40, bf16[1,256,256]{2,1,0:T(8,128)(2,1)S(1)} %all_gather.9), kind=kOutput, calls=%fused_computation | convolution fusion | flops 134479872 | bytes 1705984 | tf_op jit(solution)/shard_map/dot_general | solution.py:19
  24.7 0.5 reshape.29
  25.2 1.0 copy.9
  26.3 0.0 reduce-scatter.3.cloned.1.call-update
  26.3 0.0 reduce-scatter.5.cloned.1.call-start
  26.4 0.0 copy-start.4
  26.4 0.6 copy-done.4
  27.0 0.1 broadcast_bitcast_fusion.1
  27.1 36.6 %reduce-scatter.3.cloned.1.call-done = f32[1,128,256]{1,2,0:T(8,128)} async-done(((f32[8,128,256]{1,2,0:T(8,128)}), f32[1,128,256]{1,2,0:T(8,128)}) %reduce-scatter.3.cloned.1.call-update) | async-done | bytes 131088 | tf_op jit(solution)/shard_map/reduce_scatter | solution.py:31
  63.7 1.2 %convolution_convert_fusion = bf16[128,256]{1,0:T(8,128)(2,1)S(1)} fusion(bf16[256,256]{1,0:T(8,128)(2,1)S(1)} %copy-done, f32[1,128,256]{1,2,0:T(8,128)} %reduce-scatter.3.cloned.1.call-done, bf16[256,256]{1,0:T(8,128)(2,1)S(1)} %copy-done.3, s32[]{:T(128)S(6)} %select_n.3), kind=kOutput, calls=%fused_computation.1 | convolution fusion | flops 100761600 | bytes 393220 | tf_op jit(solution)/shard_map/dot_general | solution.py:35
  65.0 0.0 copy-start.1
  65.0 5.1 %all_gather.10 = bf16[256,256]{1,0:T(8,128)(2,1)S(1)} all-gather(bf16[128,256]{1,0:T(8,128)(2,1)S(1)} %convolution_convert_fusion), channel_id=1, replica_groups=mesh['layer'=2,'row'=4,'col'=4] {'layer'}, dimensions={0}, use_global_device_ids=true | all-gather | bytes 196608 | tf_op jit(solution)/shard_map/all_gather | solution.py:42
  70.0 7.1 %all_gather.11 = bf16[1024,256]{0,1:T(8,128)(2,1)S(1)} all-gather(bf16[256,256]{0,1:T(8,128)(2,1)S(1)} %bitcast.37), channel_id=1, replica_groups=mesh['layer'=2,'row'=4,'col'=4] {'col'}, dimensions={0}, use_global_device_ids=true | all-gather | bytes 655360 | tf_op jit(solution)/shard_map/all_gather | solution.py:47
  77.2 1.0 fusion.1
  78.2 0.0 reduce-scatter.5.cloned.1.call-update
  78.2 0.0 copy-start.2
  78.2 0.8 copy.10
  79.0 19.4 %reduce-scatter.5.cloned.1.call-done = f32[64,256]{1,0:T(8,128)} async-done(((f32[256,256]{1,0:T(8,128)}), f32[64,256]{1,0:T(8,128)}) %reduce-scatter.5.cloned.1.call-update) | async-done | bytes 65552 | tf_op jit(solution)/shard_map/reduce_scatter | solution.py:50
  98.4 1.5 %fusion.10 = bf16[1,64,256]{2,1,0:T(8,128)(2,1)} fusion(f32[64,256]{1,0:T(8,128)} %reduce-scatter.5.cloned.1.call-done, bf16[1,64,256]{2,1,0:T(8,128)(2,1)S(1)} %copy-done.2), kind=kLoop, calls=%fused_computation.14 | loop fusion | flops 49152 | bytes 131072 | tf_op jit(solution)/shard_map/reshape | solution.py:52
  (8 shorter events, 0.0 us)
Async XLA Ops:
  7.2 56.6 %copy-start = (bf16[256,256]{1,0:T(8,128)(2,1)S(1)}, bf16[256,256]{1,0:T(8,128)(2,1)}, u32[]{:S(2)}) copy-start(bf16[256,256]{1,0:T(8,128)(2,1)} %param.13) | copy-start | bytes 393220
  7.2 56.6 %reduce-scatter.3.cloned.1.call-start = ((), (), s32[]{:S(2)}) async-start(), calls=%async_computation.2 | async-start | bytes 1179648 | tf_op jit(solution)/shard_map/reduce_scatter | solution.py:31
  26.3 37.5 %copy-start.3 = (bf16[256,256]{1,0:T(8,128)(2,1)S(1)}, bf16[256,256]{1,0:T(8,128)(2,1)}, u32[]{:S(2)}) copy-start(bf16[256,256]{1,0:T(8,128)(2,1)} %param.12) | copy-start | bytes 393220
  26.3 72.1 %reduce-scatter.5.cloned.1.call-start = ((), (), s32[]{:S(2)}) async-start(), calls=%async_computation.3 | async-start | bytes 327680 | tf_op jit(solution)/shard_map/reduce_scatter | solution.py:50
  26.4 0.7 copy-start.4
  65.0 12.2 %copy-start.1 = (bf16[256,1024]{1,0:T(8,128)(2,1)S(1)}, bf16[256,1024]{1,0:T(8,128)(2,1)}, u32[]{:S(2)}) copy-start(bf16[256,1024]{1,0:T(8,128)(2,1)} %param.10) | copy-start | bytes 1572868
  78.2 20.1 %copy-start.2 = (bf16[1,64,256]{2,1,0:T(8,128)(2,1)S(1)}, bf16[1,64,256]{2,1,0:T(8,128)(2,1)}, u32[]{:S(2)}) copy-start(bf16[1,64,256]{2,1,0:T(8,128)(2,1)} %param.7) | copy-start | bytes 98308
Sparse Core Ops, SparseCore 0:
  26.4 37.2 reduce-scatter.2
  78.3 19.9 reduce-scatter.4
where the time goes:
time: 107 us
  waiting for transfers between devices  56 us (52%)
  blocking collectives  27.5 us (26%)
  between operations  14.1 us (13%)
  matrix products  3.63 us (3%)
  local copies, waits for them, and re-layouts  3.19 us (3%)
  other arithmetic  2.15 us (2%)
    reduce_scatter x1, waiting for transfers between devices, shards(): lax.psum_scatter(pieces, ('layer', 'col'), scatter_dimension=0, tiled=True)  36.6 us
    reduce_scatter x1, waiting for transfers between devices, shards(): correct = lax.psum_scatter(folded, 'row', scatter_dimension=0, tiled=True)  19.4 us
    all_gather x1, blocking collectives, shards(): lax.all_gather(leaf_sol, 'row', axis=1, tiled=True)[0]  15.3 us
    all_gather x1, blocking collectives, shards(): lax.all_gather(anc_sol, 'col', axis=0, tiled=True)  7.13 us
    all_gather x1, blocking collectives, shards(): gathered_sides = lax.all_gather(solved_part, 'layer', axis=0, tiled=True)  5.07 us
  transfers between devices with their start and end apart: 2, of which 2 were waited for; matrix products, arithmetic and copies ran while one was open for 1% of the time, Pallas kernels for 0%

commit v1 on v0

--- a/solution.py
+++ b/solution.py
@@ -1,7 +1,16 @@
+import functools
 import jax
 import jax.numpy as jnp
 from jax import lax
 from jax.sharding import PartitionSpec as P
+
+
+def treat_forms_on(local_x, dev_axis):
+    found_now = lax.all_gather(local_x, dev_axis)
+    return jnp.concatenate(found_now, axis=1)
+
+
+time_samples_all = functools.partial(treat_forms_on, dev_axis="row")
 
 
 def expand(mask, block):
@@ -17,7 +26,7 @@
     upper_masked = upper_blocks * expand(upper_mask, block).astype(jnp.bfloat16)
     columns = lower_masked
     term = lax.dot_general(
-        lax.all_gather(leaf_sol, "row", axis=1, tiled=True)[0],
+        time_samples_all(leaf_sol)[0],
         columns,
         (((0,), (1,)), ((), ())),
         preferred_element_type=jnp.float32,

time: 107 us -> 106 us (level)
  no operation moved by 1% of the time
where the time goes in v1:
time: 106 us
  waiting for transfers between devices  56.1 us (53%)
  blocking collectives  27.5 us (26%)
  between operations  14.1 us (13%)
  matrix products  3.64 us (3%)
  local copies, waits for them, and re-layouts  3.19 us (3%)
  other arithmetic  1.47 us (1%)
    reduce_scatter x1, waiting for transfers between devices, shards(): lax.psum_scatter(pieces, ('layer', 'col'), scatter_dimension=0, tiled=True)  36.7 us
    reduce_scatter x1, waiting for transfers between devices, shards(): correct = lax.psum_scatter(folded, 'row', scatter_dimension=0, tiled=True)  19.4 us
    all_gather x1, blocking collectives, treat_forms_on(): found_now = lax.all_gather(local_x, dev_axis)  15.3 us
    all_gather x1, blocking collectives, shards(): lax.all_gather(anc_sol, 'col', axis=0, tiled=True)  7.13 us
    all_gather x1, blocking collectives, shards(): gathered_sides = lax.all_gather(solved_part, 'layer', axis=0, tiled=True)  5.07 us
  transfers between devices with their start and end apart: 2, of which 2 were waited for; matrix products, arithmetic and copies ran while one was open for 1% of the time, Pallas kernels for 0%

profile of v1, /device:TPU:0, one launch (start us, length us, event | category | flops | bytes accessed | tf_op | source)
XLA Modules:
  0.0 106.0 jit_solution(8842433339759830636)
XLA Ops:
  7.2 0.0 copy-start
  7.2 0.0 reduce-scatter.3.cloned.1.call-start
  7.2 15.3 %all-gather = bf16[4,64,256]{2,1,0:T(8,128)(2,1)S(1)} all-gather(bf16[1,64,256]{2,1,0:T(8,128)(2,1)} %param.7), channel_id=2, replica_groups=mesh['layer'=2,'row'=4,'col'=4] {'row'}, dimensions={0}, use_global_device_ids=true | all-gather | bytes 163840 | tf_op jit(solution)/shard_map/all_gather | solution.py:9
  22.5 0.1 broadcast_bitcast_fusion
  22.6 1.4 %convolution_bitcast_fusion = f32[256,1024]{0,1:T(8,128)S(1)} fusion(bf16[256,256]{1,0:T(8,128)(2,1)S(1)} %bitcast.38, bf16[1024,256]{1,0:T(8,128)(2,1)} %param.8, bf16[1024]{0:T(1024)(128)(2,1)S(1)} %bitcast.40), kind=kOutput, calls=%fused_computation | convolution fusion | flops 134479872 | bytes 1705984 | tf_op jit(solution)/shard_map/dot_general | solution.py:28
  24.0 0.5 reshape.29
  24.6 1.0 copy.11
  25.6 0.0 reduce-scatter.3.cloned.1.call-update
  25.6 0.0 reduce-scatter.5.cloned.1.call-start
  25.7 0.0 copy-start.5
  25.7 0.6 copy-done.5
  26.4 0.1 broadcast_bitcast_fusion.1
  26.4 36.7 %reduce-scatter.3.cloned.1.call-done = f32[1,128,256]{1,2,0:T(8,128)} async-done(((f32[8,128,256]{1,2,0:T(8,128)}), f32[1,128,256]{1,2,0:T(8,128)}) %reduce-scatter.3.cloned.1.call-update) | async-done | bytes 131088 | tf_op jit(solution)/shard_map/reduce_scatter | solution.py:40
  63.1 0.0 copy-done.3
  63.1 1.2 %convolution_convert_fusion = bf16[128,256]{1,0:T(8,128)(2,1)S(1)} fusion(bf16[256,256]{1,0:T(8,128)(2,1)S(1)} %copy-done, f32[1,128,256]{1,2,0:T(8,128)} %reduce-scatter.3.cloned.1.call-done, bf16[256,256]{1,0:T(8,128)(2,1)S(1)} %copy-done.3, s32[]{:T(128)S(6)} %select_n.3), kind=kOutput, calls=%fused_computation.1 | convolution fusion | flops 100761600 | bytes 393220 | tf_op jit(solution)/shard_map/dot_general | solution.py:44
  64.3 0.0 copy-start.1
  64.3 5.1 %all_gather.14 = bf16[256,256]{1,0:T(8,128)(2,1)S(1)} all-gather(bf16[128,256]{1,0:T(8,128)(2,1)S(1)} %convolution_convert_fusion), channel_id=1, replica_groups=mesh['layer'=2,'row'=4,'col'=4] {'layer'}, dimensions={0}, use_global_device_ids=true | all-gather | bytes 196608 | tf_op jit(solution)/shard_map/all_gather | solution.py:51
  69.4 7.1 %all_gather.15 = bf16[1024,256]{0,1:T(8,128)(2,1)S(1)} all-gather(bf16[256,256]{0,1:T(8,128)(2,1)S(1)} %bitcast.36), channel_id=1, replica_groups=mesh['layer'=2,'row'=4,'col'=4] {'col'}, dimensions={0}, use_global_device_ids=true | all-gather | bytes 655360 | tf_op jit(solution)/shard_map/all_gather | solution.py:56
  76.5 1.0 fusion.1
  77.6 0.0 reduce-scatter.5.cloned.1.call-update
  77.6 0.0 copy-start.2
  77.6 0.8 copy.12
  78.4 19.4 %reduce-scatter.5.cloned.1.call-done = f32[64,256]{1,0:T(8,128)} async-done(((f32[256,256]{1,0:T(8,128)}), f32[64,256]{1,0:T(8,128)}) %reduce-scatter.5.cloned.1.call-update) | async-done | bytes 65552 | tf_op jit(solution)/shard_map/reduce_scatter | solution.py:59
  97.7 1.5 %fusion.9 = bf16[1,64,256]{2,1,0:T(8,128)(2,1)} fusion(f32[64,256]{1,0:T(8,128)} %reduce-scatter.5.cloned.1.call-done, bf16[1,64,256]{2,1,0:T(8,128)(2,1)S(1)} %copy-done.2), kind=kLoop, calls=%fused_computation.13 | loop fusion | flops 49152 | bytes 131072 | tf_op jit(solution)/shard_map/reshape | solution.py:61
  (10 shorter events, 0.0 us)
Async XLA Ops:
  7.2 55.9 %copy-start = (bf16[256,256]{1,0:T(8,128)(2,1)S(1)}, bf16[256,256]{1,0:T(8,128)(2,1)}, u32[]{:S(2)}) copy-start(bf16[256,256]{1,0:T(8,128)(2,1)} %param.13) | copy-start | bytes 393220
  7.2 15.4 %copy-start.4 = (s32[4,1]{0,1:T(1,128)S(1)}, s32[4,1]{0,1:T(1,128)}, u32[]{:S(2)}) copy-start(s32[4,1]{0,1:T(1,128)} %param.9) | copy-start | bytes 52
  7.2 55.9 %reduce-scatter.3.cloned.1.call-start = ((), (), s32[]{:S(2)}) async-start(), calls=%async_computation.2 | async-start | bytes 1179648 | tf_op jit(solution)/shard_map/reduce_scatter | solution.py:40
  25.6 37.5 %copy-start.3 = (bf16[256,256]{1,0:T(8,128)(2,1)S(1)}, bf16[256,256]{1,0:T(8,128)(2,1)}, u32[]{:S(2)}) copy-start(bf16[256,256]{1,0:T(8,128)(2,1)} %param.12) | copy-start | bytes 393220
  25.6 72.1 %reduce-scatter.5.cloned.1.call-start = ((), (), s32[]{:S(2)}) async-start(), calls=%async_computation.3 | async-start | bytes 327680 | tf_op jit(solution)/shard_map/reduce_scatter | solution.py:59
  25.7 0.7 copy-start.5
  64.3 12.2 %copy-start.1 = (bf16[256,1024]{1,0:T(8,128)(2,1)S(1)}, bf16[256,1024]{1,0:T(8,128)(2,1)}, u32[]{:S(2)}) copy-start(bf16[256,1024]{1,0:T(8,128)(2,1)} %param.10) | copy-start | bytes 1572868
  77.6 20.1 %copy-start.2 = (bf16[1,64,256]{2,1,0:T(8,128)(2,1)S(1)}, bf16[1,64,256]{2,1,0:T(8,128)(2,1)}, u32[]{:S(2)}) copy-start(bf16[1,64,256]{2,1,0:T(8,128)(2,1)} %param.7) | copy-start | bytes 98308
Sparse Core Ops, SparseCore 0:
  25.8 37.2 reduce-scatter.2
  77.7 19.9 reduce-scatter.4
